TPU v7x, 32 devices: a whole 2x2x4 slice. The times are simulated.
32 devices in a mesh: ctx: 16 (over z, y, x), tp: 2 (over core).
Axes of the slice: x: 2, y: 2, z: 4, core: 2. Of those that a mesh axis runs over, the one named last changes fastest.
Arguments:
- ssm_input: bfloat16 [2048, 8192], P('ctx', 'tp'), may hold values from -40 to 40
- ssm_gate: bfloat16 [2048, 8192], P('ctx', 'tp'), may hold values from -4 to 4
- state_write: bfloat16 [2048, 128], P('ctx'), may hold values from -0.5 to 0.5
- state_read: bfloat16 [2048, 128], P('ctx'), may hold values from -0.5 to 0.5
- log_decay: float32 [2048, 32], P('ctx', 'tp'), may hold values from -4 to 0
- skip_gain: float32 [32], P('tp'), may hold values from 0.5 to 1.5
- norm_gain: float32 [8192], P('tp'), may hold values from 0.1 to 1.9
- ssm_cotangent: bfloat16 [2048, 8192], P('ctx', 'tp'), may hold values from -6 to 6
- queries: bfloat16 [2048, 8192], P('ctx', 'tp'), may hold values from -5 to 5
- key_states: bfloat16 [2048, 1024], P('ctx', 'tp'), may hold values from -5 to 5
- value_states: bfloat16 [2048, 1024], P('ctx', 'tp'), may hold values from -6 to 6
- attn_cotangent: bfloat16 [2048, 8192], P('ctx', 'tp'), may hold values from -6 to 6
Outputs:
- ssm_output: bfloat16 [2048, 8192], P('ctx', 'tp')
- input_grad: bfloat16 [2048, 8192], P('ctx', 'tp')
- gate_grad: bfloat16 [2048, 8192], P('ctx', 'tp')
- write_grad: float32 [2048, 128], P('ctx')
- read_grad: float32 [2048, 128], P('ctx')
- attn_output: bfloat16 [2048, 8192], P('ctx', 'tp')
- query_grad: bfloat16 [2048, 8192], P('ctx', 'tp')
- key_grad: bfloat16 [2048, 1024], P('ctx', 'tp')
- value_grad: bfloat16 [2048, 1024], P('ctx', 'tp')
All inputs are finite; a program needn't handle non-finite values.
Results may differ from a plain program's by a relative error of at most 0.035.
Values may be sent and summed in bfloat16 or wider, within the bound.
A program may use at most 192 MiB of HBM per device.

v0:
```python
import jax
import jax.numpy as jnp
from jax import lax
from jax.sharding import PartitionSpec as P

HD = 128
CH = 8192
PRECISE = lax.Precision.HIGHEST
NEGATIVE = -1e30
EPSILON = 1e-05
TILE_KEYS = 1024


def carried_in(x, axis, join, neutral, backward):
    count = lax.axis_size(axis)
    place = lax.axis_index(axis)
    ahead = count - 1 - place if backward else place
    gathered = jax.tree.map(
        lambda a, kind: lax.all_gather(a.astype(kind), axis),
        x,
        jax.tree.map(lambda a: jnp.bfloat16 if a.dtype == jnp.float32 else a.dtype, x),
    )
    state = jax.tree.map(lambda a, e: jnp.zeros_like(a) + jnp.asarray(e, a.dtype), x, neutral)

    def one(turn, state):
        source = count - 1 - turn if backward else turn
        return join(
            state,
            jax.tree.map(
                lambda a, own: lax.dynamic_index_in_dim(a, source, 0, False).astype(own.dtype),
                gathered,
                x,
            ),
        )

    return lax.fori_loop(0, ahead, one, state)


def for_sending(x):

    def short(part):
        return part.astype(jnp.bfloat16) if part.dtype == jnp.float32 else part

    return jax.tree.map(short, x)


def spread(value, axis, source):
    kept = jnp.where(lax.axis_index(axis) == source, value, 0).astype(value.dtype)
    return lax.psum(kept, axis)


def combine(earlier, latter):
    return (earlier[0] * latter[0], latter[0][:, None, None] * earlier[1] + latter[1])


def carried(leading, trailing):
    neutral = (jnp.ones_like(leading[0]), jnp.zeros_like(leading[1]))
    before_state = carried_in(leading, "ctx", combine, neutral, False)
    through = combine(before_state, leading)
    total_state = spread(for_sending(through[1]), "ctx", lax.axis_size("ctx") - 1)
    after_state = carried_in(trailing, "ctx", combine, neutral, True)
    entering = after_state[0][:, None, None] * total_state + after_state[1]
    return (before_state[1], entering)


def ssm_layer(
    ssm_input, ssm_gate, state_write, state_read, log_decay, skip_gain, norm_gain, ssm_cotangent
):
    tok_rows, channel_count = ssm_input.shape
    head_count = log_decay.shape[1]
    half_rows = tok_rows // 2
    head_dim = channel_count // head_count
    input_f32 = ssm_input.astype(jnp.float32).reshape(2, half_rows, head_count, head_dim)
    write_pair = state_write.reshape(2, half_rows, -1)
    read_pair = state_read.reshape(2, half_rows, -1)
    write_f32 = write_pair.astype(jnp.float32)
    read_f32 = read_pair.astype(jnp.float32)
    log_total = jnp.cumsum(log_decay.reshape(2, half_rows, head_count), axis=1)
    by_head = jnp.transpose(log_total, (0, 2, 1))
    log_gap = by_head[:, :, :, None] - by_head[:, :, None, :]
    causal = lax.broadcasted_iota(jnp.int32, (half_rows, half_rows), 0) >= lax.broadcasted_iota(
        jnp.int32, (half_rows, half_rows), 1
    )
    decay = jnp.exp(jnp.where(causal, log_gap, NEGATIVE))
    read_write = jnp.einsum(
        "ctn,csn->cts", read_pair, write_pair, preferred_element_type=jnp.float32
    )
    weights = decay * read_write[:, None, :, :]
    grow_in = jnp.exp(log_total)
    log_last = log_total[:, -1, :]
    shrink = jnp.exp(log_last[:, None, :] - log_total)
    block_decay = jnp.exp(log_last)
    local_state = jnp.einsum(
        "cshp,csn->chpn", input_f32 * shrink[..., None], write_f32, precision=PRECISE
    )
    first_in, second_in = carried(
        (block_decay[0], local_state[0]), (block_decay[1], local_state[1])
    )
    state_in = jnp.stack([first_in, second_in])
    mixed = jnp.einsum("chts,cshp->cthp", weights, input_f32, precision=PRECISE)
    mixed = mixed + grow_in[..., None] * jnp.einsum(
        "chpn,ctn->cthp", state_in, read_f32, precision=PRECISE
    )
    mixed = mixed + skip_gain[None, None, :, None] * input_f32
    mixed = mixed.reshape(tok_rows, channel_count)
    gate_f32 = ssm_gate.astype(jnp.float32)
    sigmoid_gate = jax.nn.sigmoid(gate_f32)
    gated = mixed * gate_f32 * sigmoid_gate
    square_sum = lax.psum(jnp.sum(gated * gated, axis=1), "tp")
    root_mean = jnp.sqrt(square_sum / CH + EPSILON)[:, None]
    normed = gated / root_mean
    ssm_output = (normed * norm_gain).astype(jnp.bfloat16)
    d_normed = ssm_cotangent.astype(jnp.float32) * norm_gain
    inner_sum = lax.psum(jnp.sum(d_normed * normed, axis=1), "tp")
    d_gated = (d_normed - normed * (inner_sum / CH)[:, None]) / root_mean
    d_mixed_flat = d_gated * gate_f32 * sigmoid_gate
    gate_grad = (d_gated * mixed * sigmoid_gate * (1.0 + gate_f32 * (1.0 - sigmoid_gate))).astype(
        jnp.bfloat16
    )
    d_mixed = d_mixed_flat.reshape(2, half_rows, head_count, head_dim)
    local_adjoint = jnp.einsum(
        "cshp,csn->chpn", d_mixed * grow_in[..., None], read_f32, precision=PRECISE
    )
    second_back, first_back = carried(
        (block_decay[1], local_adjoint[1]), (block_decay[0], local_adjoint[0])
    )
    adjoint_in = jnp.stack([first_back, second_back])
    input_g = jnp.einsum("chst,cshp->cthp", weights, d_mixed, precision=PRECISE)
    input_g = input_g + shrink[..., None] * jnp.einsum(
        "chpn,ctn->cthp", adjoint_in, write_f32, precision=PRECISE
    )
    input_g = input_g + skip_gain[None, None, :, None] * d_mixed
    input_grad = input_g.reshape(tok_rows, channel_count).astype(jnp.bfloat16)
    dot_pairs = jnp.einsum("cthp,cshp->chts", d_mixed, input_f32, precision=PRECISE)
    kernel = jnp.sum(decay * dot_pairs, axis=1)
    read_g = jnp.einsum("cts,csn->ctn", kernel, write_f32, precision=PRECISE)
    read_g = read_g + jnp.einsum(
        "cthp,chpn->ctn", d_mixed * grow_in[..., None], state_in, precision=PRECISE
    )
    write_g = jnp.einsum("cst,csn->ctn", kernel, read_f32, precision=PRECISE)
    write_g = write_g + jnp.einsum(
        "cthp,chpn->ctn", input_f32 * shrink[..., None], adjoint_in, precision=PRECISE
    )
    write_grad, read_grad = (
        lax.psum(write_g.reshape(tok_rows, -1).astype(jnp.bfloat16), "tp").astype(jnp.float32),
        lax.psum(read_g.reshape(tok_rows, -1).astype(jnp.bfloat16), "tp").astype(jnp.float32),
    )
    return (ssm_output, input_grad, gate_grad, write_grad, read_grad)


def pick_half(values, half_id):
    return lax.dynamic_index_in_dim(values, half_id, 0, keepdims=False)


def take_half(tree, half_id):
    return jax.tree.map(lambda values: pick_half(values, half_id), tree)


def put_half(tree, half_id, update_tree):
    return jax.tree.map(
        lambda values, replacement: lax.dynamic_update_index_in_dim(
            values, replacement, half_id, 0
        ),
        tree,
        update_tree,
    )


def add_rows(totals, update_rows, row_start):
    current = lax.dynamic_slice_in_dim(totals, row_start, update_rows.shape[0], 0)
    return lax.dynamic_update_slice_in_dim(totals, current + update_rows, row_start, 0)


def score_block(query_block, key_block, key_mask, score_scale):
    raw_scores = (
        jnp.einsum("tkgd,skd->kgts", query_block, key_block, preferred_element_type=jnp.float32)
        * score_scale
    )
    return jnp.where(key_mask, raw_scores, NEGATIVE)


def absorb(soft_state, query_block, key_block, value_block, key_mask, score_scale):
    row_max, weight_sum, accum_out = soft_state
    scores = score_block(query_block, key_block, key_mask, score_scale)
    new_max = jnp.maximum(row_max, jnp.max(scores, axis=-1))
    rescale = jnp.exp(row_max - new_max)
    prob_full = jnp.exp(scores - new_max[..., None])
    accum_out = accum_out * rescale[..., None] + jnp.einsum(
        "kgts,skd->kgtd",
        prob_full.astype(jnp.bfloat16),
        value_block,
        preferred_element_type=jnp.float32,
    )
    return (new_max, weight_sum * rescale + jnp.sum(prob_full, axis=-1), accum_out)


def grad_block(
    query_block, key_block, value_block, cot_block, norm_block, delta_block, key_mask, score_scale
):
    scores = score_block(query_block, key_block, key_mask, score_scale)
    prob_full = jnp.exp(scores - norm_block[..., None])
    weights = prob_full.astype(jnp.bfloat16)
    d_prob = jnp.einsum(
        "tkgd,skd->kgts", cot_block, value_block, preferred_element_type=jnp.float32
    )
    d_score = (prob_full * (d_prob - delta_block[..., None]) * score_scale).astype(jnp.bfloat16)
    query_g = jnp.einsum("kgts,skd->tkgd", d_score, key_block, preferred_element_type=jnp.float32)
    key_g = jnp.einsum("kgts,tkgd->skd", d_score, query_block, preferred_element_type=jnp.float32)
    value_g = jnp.einsum("kgts,tkgd->skd", weights, cot_block, preferred_element_type=jnp.float32)
    return (query_g, key_g, value_g)


def key_positions(first_row, row_count, tok_rows, half_rows, ctx_count):
    row_id = first_row + lax.iota(jnp.int32, row_count)
    device_id = row_id // tok_rows
    local_id = row_id % tok_rows
    block_id = jnp.where(local_id < half_rows, device_id, 2 * ctx_count - 1 - device_id)
    return block_id * half_rows + local_id % half_rows


def over_pieces(by_rows, carry, pieces, tok_rows):
    row_count = pieces[0].shape[0]
    shards = row_count // tok_rows
    group = 1
    for candidate in range(1, shards + 1):
        if shards % candidate == 0 and candidate * tok_rows <= TILE_KEYS:
            group = candidate
    tile_rows = group * tok_rows

    def tile_turn(offset, inner_carry):
        key_rows = lax.dynamic_slice_in_dim(pieces[0], offset * tile_rows, tile_rows, 0)
        value_rows = lax.dynamic_slice_in_dim(pieces[1], offset * tile_rows, tile_rows, 0)
        return by_rows(inner_carry, key_rows, value_rows, offset * tile_rows)

    return lax.fori_loop(0, shards // group, tile_turn, carry)


def attention(queries, key_states, value_states, attn_cotangent):
    tok_rows = queries.shape[0]
    half_rows = tok_rows // 2
    kv_count = key_states.shape[1] // HD
    group_size = queries.shape[1] // HD // kv_count
    score_scale = HD ** (-0.5)
    ctx_count = lax.axis_size("ctx")
    own_index = lax.axis_index("ctx")
    query_pair = queries.reshape(2, half_rows, kv_count, group_size, HD)
    cot_pair = attn_cotangent.reshape(2, half_rows, kv_count, group_size, HD)
    block_starts = jnp.stack([own_index, 2 * ctx_count - 1 - own_index]) * half_rows
    query_pos = block_starts[:, None] + lax.iota(jnp.int32, half_rows)[None, :]

    def forward_rows(soft_state, key_rows, value_rows, first_row):
        row_count = key_rows.shape[0]
        key_pos = key_positions(first_row, row_count, tok_rows, half_rows, ctx_count)
        key_block = key_rows.reshape(row_count, kv_count, HD)
        value_block = value_rows.reshape(row_count, kv_count, HD)
        for half_id in range(2):
            key_mask = key_pos[None, :] <= query_pos[half_id][:, None]
            soft_state = put_half(
                soft_state,
                half_id,
                absorb(
                    take_half(soft_state, half_id),
                    query_pair[half_id],
                    key_block,
                    value_block,
                    key_mask,
                    score_scale,
                ),
            )
        return soft_state

    start_state = (
        jnp.full((2, kv_count, group_size, half_rows), NEGATIVE, jnp.float32),
        jnp.zeros((2, kv_count, group_size, half_rows), jnp.float32),
        jnp.zeros((2, kv_count, group_size, half_rows, HD), jnp.float32),
    )
    row_max, weight_sum, accum_out = over_pieces(
        forward_rows,
        start_state,
        (
            lax.all_gather(key_states, "ctx", axis=0, tiled=True),
            lax.all_gather(value_states, "ctx", axis=0, tiled=True),
        ),
        tok_rows,
    )
    out_pair = jnp.transpose(accum_out / weight_sum[..., None], (0, 3, 1, 2, 4))
    attn_output = out_pair.reshape(tok_rows, -1).astype(jnp.bfloat16)
    norm_pair = row_max + jnp.log(weight_sum)
    delta_rows = jnp.sum(
        attn_output.reshape(2, half_rows, kv_count, group_size, HD).astype(jnp.float32)
        * cot_pair.astype(jnp.float32),
        axis=-1,
    )
    delta_pair = jnp.transpose(delta_rows, (0, 2, 3, 1))

    def backward_rows(carry, key_rows, value_rows, first_row):
        row_count = key_rows.shape[0]
        key_pos = key_positions(first_row, row_count, tok_rows, half_rows, ctx_count)
        key_block = key_rows.reshape(row_count, kv_count, HD)
        value_block = value_rows.reshape(row_count, kv_count, HD)
        dq_pair, dk_all, dv_all = carry
        for half_id in range(2):
            key_mask = key_pos[None, :] <= query_pos[half_id][:, None]
            block_grads = grad_block(
                query_pair[half_id],
                key_block,
                value_block,
                cot_pair[half_id],
                norm_pair[half_id],
                delta_pair[half_id],
                key_mask,
                score_scale,
            )
            dq_pair = dq_pair.at[half_id].add(block_grads[0])
            dk_all = add_rows(dk_all, block_grads[1], first_row)
            dv_all = add_rows(dv_all, block_grads[2], first_row)
        return (dq_pair, dk_all, dv_all)

    all_rows = tok_rows * ctx_count
    grad_start = (
        jnp.zeros((2, half_rows, kv_count, group_size, HD), jnp.float32),
        jnp.zeros((all_rows, kv_count, HD), jnp.float32),
        jnp.zeros((all_rows, kv_count, HD), jnp.float32),
    )
    dq_pair, dk_all, dv_all = over_pieces(
        backward_rows,
        grad_start,
        (
            lax.all_gather(key_states, "ctx", axis=0, tiled=True),
            lax.all_gather(value_states, "ctx", axis=0, tiled=True),
        ),
        tok_rows,
    )
    dk_mine, dv_mine = (
        lax.psum_scatter(
            dk_all.astype(jnp.bfloat16), "ctx", scatter_dimension=0, tiled=True
        ).astype(jnp.float32),
        lax.psum_scatter(
            dv_all.astype(jnp.bfloat16), "ctx", scatter_dimension=0, tiled=True
        ).astype(jnp.float32),
    )
    query_grad = dq_pair.reshape(tok_rows, -1).astype(jnp.bfloat16)
    key_grad = dk_mine.reshape(tok_rows, -1).astype(jnp.bfloat16)
    value_grad = dv_mine.reshape(tok_rows, -1).astype(jnp.bfloat16)
    return (attn_output, query_grad, key_grad, value_grad)


def per_device(
    ssm_input,
    ssm_gate,
    state_write,
    state_read,
    log_decay,
    skip_gain,
    norm_gain,
    ssm_cotangent,
    queries,
    key_states,
    value_states,
    attn_cotangent,
):
    ssm_results = ssm_layer(
        ssm_input, ssm_gate, state_write, state_read, log_decay, skip_gain, norm_gain, ssm_cotangent
    )
    attn_results = attention(queries, key_states, value_states, attn_cotangent)
    return ssm_results + attn_results


def solution(mesh):
    placed = (
        P("ctx", "tp"),
        P("ctx", "tp"),
        P("ctx", None),
        P("ctx", None),
        P("ctx", "tp"),
        P("tp"),
        P("tp"),
        P("ctx", "tp"),
        P("ctx", "tp"),
        P("ctx", "tp"),
        P("ctx", "tp"),
        P("ctx", "tp"),
    )
    return jax.shard_map(
        per_device,
        mesh=mesh,
        in_specs=placed,
        out_specs=(
            P("ctx", "tp"),
            P("ctx", "tp"),
            P("ctx", "tp"),
            P("ctx", None),
            P("ctx", None),
            P("ctx", "tp"),
            P("ctx", "tp"),
            P("ctx", "tp"),
            P("ctx", "tp"),
        ),
        check_vma=False,
    )
```

profile of v0, /device:TPU:0, one launch (start us, length us, event | category | flops | bytes accessed | tf_op | source)
XLA Modules:
  0.0 1338.4 jit_solution(10396937734925266200)
XLA Ops:
  13.3 3.8 fusion.126
  21.1 42.3 %all-gather = bf16[16,1,16]{2,1,0:T(2,128)(2,1)S(1)} all-gather(bf16[1,1,16]{2,1,0:T(2,128)(2,1)S(1)} %get-tuple-element.1035), channel_id=1, replica_groups=mesh['ctx'=16,'tp'=2] {'ctx'}, dimensions={0}, use_global_device_ids=true | all-gather | bytes 544 | tf_op jit(solution)/shard_map/all_gather | solution.py:19
  68.1 9.3 all-gather.17.cloned.1.call-done
  77.4 64.8 %all-gather.19.cloned.1.call-done = bf16[2048,512]{0,1:T(8,128)(2,1)} async-done(((bf16[128,512]{0,1:T(8,128)(2,1)}), bf16[2048,512]{0,1:T(8,128)(2,1)}) %all-gather.19.cloned.1.call-update) | async-done | bytes 2097168 | tf_op jit(solution)/shard_map/all_gather | solution.py:282
  142.4 28.6 %while.98 = (s32[]{:T(128)}, f32[2,4,8,64]{3,2,1,0:T(8,128)S(1)}, f32[2,4,8,64]{3,2,1,0:T(8,128)S(1)}, f32[2,4,8,64,128]{4,3,2,1,0:T(8,128)S(1)}, s32[2,64]{1,0:...) while((s32[]{:T(128)}, f32[2,4,8,64]{3,2,1,0:T(8,128)S(1)}, ...), condition=%wide.region_23.24_spmd, body=%wide.region_18.23_spmd.sunk | while | flops 2194853888 | bytes 69060272 | solution.py:235
  171.8 4.3 multiply_reduce_fusion
  177.8 157.5 %all-gather.9.cloned.1.call-done = bf16[16,16,256,128]{3,2,1,0:T(8,128)(2,1)} async-done(((bf16[1,16,256,128]{3,2,1,0:T(8,128)(2,1)}), bf16[16,16,256,128]{3,2,1,0:T(8,128)(2,1)}) %all-gather.9.cloned.1.call-update) | async-done | bytes 16777232 | tf_op jit(solution)/shard_map/all_gather | solution.py:19
  335.5 3.7 fusion.164
  344.1 65.2 %while.99 = (s32[]{:T(128)}, f32[2,64,4,8,128]{4,1,3,2,0:T(8,128)S(1)}, f32[2048,4,128]{2,0,1:T(8,128)}, f32[2048,4,128]{2,0,1:T(8,128)}, bf16[2048,512]{0,1:T(8...) while((s32[]{:T(128)}, ...), condition=%wide.region_26.27_spmd, body=%wide.region_25.26_spmd.sunk | while | flops 5417635840 | bytes 150054832 | solution.py:235
  363.3 7.4 fusion.328
  370.8 5.9 fusion.329
  395.7 7.5 fusion.328
  403.2 5.9 fusion.329
  409.3 4.0 convert_element_type.295
  414.2 66.9 %all-gather.1 = bf16[16,1,16]{2,1,0:T(2,128)(2,1)S(1)} all-gather(bf16[1,1,16]{2,1,0:T(2,128)(2,1)S(1)} %copy-done.38), channel_id=1, replica_groups=mesh['ctx'=16,'tp'=2] {'ctx'}, dimensions={0}, use_global_device_ids=true | all-gather | bytes 544 | tf_op jit(solution)/shard_map/all_gather | solution.py:19
  484.1 3.8 convert_element_type.297
  488.0 40.5 %all-gather.11.cloned.1.call-done = bf16[16,16,256,128]{3,2,1,0:T(8,128)(2,1)} async-done(((bf16[1,16,256,128]{3,2,1,0:T(8,128)(2,1)}), bf16[16,16,256,128]{3,2,1,0:T(8,128)(2,1)}) %all-gather.11.cloned.1.call-update) | async-done | bytes 16777232 | tf_op jit(solution)/shard_map/all_gather | solution.py:19
  530.1 53.4 %while.95 = (s32[]{:T(128)}, f32[16]{0:T(128)S(1)}, f32[16,256,128]{2,1,0:T(8,128)}, s32[]{:T(128)}, bf16[16,16]{1,0:T(8,128)(2,1)S(1)}, /*index=5*/bf16[16,16,2...) while((s32[]{:T(128)}, f32[16]{0:T(128)S(1)}, f32[16,256,128]{2,1,0:T(8,128)}, ...), condition=%wide.region_4.5_spmd, body=%wide.region_3.4_spmd.sunk | while | flops 1572902 | bytes 5243331 | solution.py:36
  537.1 3.7 convert_add_fusion.9
  547.9 3.5 convert_add_fusion.9
  551.5 3.6 convert_add_fusion.9
  555.1 3.5 convert_add_fusion.9
  562.2 3.5 convert_add_fusion.9
  565.7 3.5 convert_add_fusion.9
  572.8 3.6 convert_add_fusion.9
  583.5 60.7 %all-reduce.5.cloned.1.call-done = bf16[16,256,128]{2,1,0:T(8,128)(2,1)} async-done(((bf16[16,256,128]{2,1,0:T(8,128)(2,1)}), bf16[16,256,128]{2,1,0:T(8,128)(2,1)}) %all-reduce.5.cloned.1.call-update) | async-done | bytes 1048592 | tf_op jit(solution)/shard_map/psum | solution.py:49
  658.1 4.1 multiply_reduce_fusion.1
  664.6 5.2 fusion.135
  671.9 4.4 fusion.144
  683.7 42.3 %reduce-scatter.3.cloned.1.call-done = bf16[128,4,128]{2,0,1:T(8,128)(2,1)} async-done(((bf16[2048,4,128]{2,0,1:T(8,128)(2,1)}), bf16[128,4,128]{2,0,1:T(8,128)(2,1)}) %reduce-scatter.3.cloned.1.call-update) | async-done | bytes 131088 | tf_op jit(solution)/shard_map/reduce_scatter | solution.py:335
  727.5 78.9 %reduce-scatter.5.cloned.1.call-done = bf16[128,4,128]{2,0,1:T(8,128)(2,1)} async-done(((bf16[2048,4,128]{2,0,1:T(8,128)(2,1)}), bf16[128,4,128]{2,0,1:T(8,128)(2,1)}) %reduce-scatter.5.cloned.1.call-update) | async-done | bytes 131088 | tf_op jit(solution)/shard_map/reduce_scatter | solution.py:338
  808.0 6.1 fusion.158
  817.5 4.7 fusion.150
  822.1 175.3 %all-gather.15.cloned.1.call-done = bf16[16,16,256,128]{3,2,1,0:T(8,128)(2,1)} async-done(((bf16[1,16,256,128]{3,2,1,0:T(8,128)(2,1)}), bf16[16,16,256,128]{3,2,1,0:T(8,128)(2,1)}) %all-gather.15.cloned.1.call-update) | async-done | bytes 16777232 | tf_op jit(solution)/shard_map/all_gather | solution.py:19
  1001.4 188.7 %all-gather.13.cloned.1.call-done = bf16[16,16,256,128]{3,2,1,0:T(8,128)(2,1)} async-done(((bf16[1,16,256,128]{3,2,1,0:T(8,128)(2,1)}), bf16[16,16,256,128]{3,2,1,0:T(8,128)(2,1)}) %all-gather.13.cloned.1.call-update) | async-done | bytes 16777232 | tf_op jit(solution)/shard_map/all_gather | solution.py:19
  1191.6 63.5 %while.96 = (s32[]{:T(128)}, f32[16]{0:T(128)S(1)}, f32[16,256,128]{2,1,0:T(8,128)}, s32[]{:T(128)}, bf16[16,16]{1,0:T(8,128)(2,1)}, /*index=5*/bf16[16,16,256,1...) while((s32[]{:T(128)}, f32[16]{0:T(128)S(1)}, f32[16,256,128]{2,1,0:T(8,128)}, ...), condition=%wide.region_11.12_spmd, body=%wide.region_10.11_spmd.sunk | while | flops 1572902 | bytes 5243331 | solution.py:36
  1204.9 3.5 convert_add_fusion.10
  1209.1 3.6 convert_add_fusion.10
  1213.4 3.5 convert_add_fusion.10
  1217.6 3.6 convert_add_fusion.10
  1226.1 3.6 convert_add_fusion.10
  1230.4 3.5 convert_add_fusion.10
  1234.6 3.6 convert_add_fusion.10
  1243.1 3.5 convert_add_fusion.10
  1251.6 3.5 convert_add_fusion.10
  1255.1 50.6 %all-reduce.7.cloned.1.call-done = bf16[16,256,128]{2,1,0:T(8,128)(2,1)} async-done(((bf16[16,256,128]{2,1,0:T(8,128)(2,1)}), bf16[16,256,128]{2,1,0:T(8,128)(2,1)}) %all-reduce.7.cloned.1.call-update) | async-done | bytes 1048592 | tf_op jit(solution)/shard_map/psum | solution.py:49
  1311.9 6.3 fusion.138
  1320.3 8.7 all-reduce.9.cloned.1.call-done
  (285 shorter events, 201.9 us)
Async XLA Ops:
  7.2 474.0 %copy-start = (bf16[128,128]{1,0:T(8,128)(2,1)S(1)}, bf16[128,128]{1,0:T(8,128)(2,1)}, u32[]{:S(2)}) copy-start(bf16[128,128]{1,0:T(8,128)(2,1)} %param.31) | copy-start | bytes 98308
  7.2 5.0 copy-start.36
  7.2 6.1 copy-start.26
  7.2 70.1 %all-gather.17.cloned.1.call-start = ((), (), s32[]{:S(2)}) async-start(), calls=%async_computation.8 | async-start | bytes 2228224 | tf_op jit(solution)/shard_map/all_gather | solution.py:281
  8.9 133.2 %all-gather.19.cloned.1.call-start = ((), (), s32[]{:S(2)}) async-start(), calls=%async_computation.9 | async-start | bytes 2228224 | tf_op jit(solution)/shard_map/all_gather | solution.py:282
  10.7 324.6 %all-gather.9.cloned.1.call-start = ((), (), s32[]{:S(2)}) async-start(), calls=%async_computation.2 | async-start | bytes 17825792 | tf_op jit(solution)/shard_map/all_gather | solution.py:19
  12.2 4.9 copy-start.9
  12.4 4.7 copy-start.24
  13.3 3.8 copy-start.30
  17.1 2.6 copy-start.14
  19.8 43.6 %copy-start.22 = (bf16[128,4096]{1,0:T(8,128)(2,1)S(1)}, bf16[128,4096]{1,0:T(8,128)(2,1)}, u32[]{:S(2)}) copy-start(bf16[128,4096]{1,0:T(8,128)(2,1)} %param.39) | copy-start | bytes 3145732
  19.8 508.7 %all-gather.11.cloned.1.call-start = ((), (), s32[]{:S(2)}) async-start(), calls=%async_computation.3 | async-start | bytes 17825792 | tf_op jit(solution)/shard_map/all_gather | solution.py:19
  20.4 623.8 %all-reduce.5.cloned.1.call-start = ((), (), s32[]{:S(2)}) async-start(), calls=%async_computation.4 | async-start | bytes 2097152 | tf_op jit(solution)/shard_map/psum | solution.py:49
  63.6 2.3 copy-start.16
  335.5 3.8 copy-start.3
  335.5 3.7 copy-start.34
  339.3 386.7 %reduce-scatter.3.cloned.1.call-start = ((), (), s32[]{:S(2)}) async-start(), calls=%async_computation.10 | async-start | bytes 2228224 | tf_op jit(solution)/shard_map/reduce_scatter | solution.py:335
  346.6 2.2 copy-start.23
  348.6 3.3 copy-start.29
  348.6 5.9 copy-start.28
  348.7 3.1 copy-start.21
  348.8 5.8 copy-start.20
  363.3 7.5 copy-start.2
  379.0 2.2 copy-start.23
  381.0 3.3 copy-start.29
  381.0 5.9 copy-start.28
  381.2 3.1 copy-start.21
  381.2 5.8 copy-start.20
  395.7 7.5 copy-start.2
  413.3 67.8 %copy-start.32 = (f32[2,64,16]{2,1,0:T(8,128)S(1)}, f32[2,64,16]{2,1,0:T(8,128)}, u32[]{:S(2)}) copy-start(f32[2,64,16]{2,1,0:T(8,128)} %get-tuple-element.1031) | copy-start | bytes 24580
  413.3 67.9 %copy-start.27 = (bf16[128,128]{1,0:T(8,128)(2,1)S(1)}, bf16[128,128]{1,0:T(8,128)(2,1)}, u32[]{:S(2)}) copy-start(bf16[128,128]{1,0:T(8,128)(2,1)} %param.30) | copy-start | bytes 98308
  413.3 68.0 %copy-start.10 = (bf16[16,8,16,256]{3,2,1,0:T(8,128)(2,1)S(1)}, bf16[16,8,16,256]{3,2,1,0:T(8,128)(2,1)}, u32[]{:S(2)}) copy-start(bf16[16,8,16,256]{3,2,1,0:T(8,128)(2,1)} %copy-done.9) | copy-start | bytes 3145732
  413.3 393.0 %reduce-scatter.5.cloned.1.call-start = ((), (), s32[]{:S(2)}) async-start(), calls=%async_computation.11 | async-start | bytes 2228224 | tf_op jit(solution)/shard_map/reduce_scatter | solution.py:338
  487.9 509.5 %all-gather.15.cloned.1.call-start = ((), (), s32[]{:S(2)}) async-start(), calls=%async_computation.6 | async-start | bytes 17825792 | tf_op jit(solution)/shard_map/all_gather | solution.py:19
  644.2 2.5 copy-start.4
  644.2 3.2 copy-start.18
  644.2 3.2 copy-start.35
  646.5 4.1 copy-start.12
  651.8 3.0 copy-start.17
  653.5 4.6 copy-start.33
  676.3 2.7 copy-start.15
  679.0 511.0 %all-gather.13.cloned.1.call-start = ((), (), s32[]{:S(2)}) async-start(), calls=%async_computation.5 | async-start | bytes 17825792 | tf_op jit(solution)/shard_map/all_gather | solution.py:19
  679.8 625.9 %all-reduce.7.cloned.1.call-start = ((), (), s32[]{:S(2)}) async-start(), calls=%async_computation.7 | async-start | bytes 2097152 | tf_op jit(solution)/shard_map/psum | solution.py:49
  681.7 126.3 %copy-start.5 = (f32[16,256,128]{2,1,0:T(8,128)S(1)}, f32[16,256,128]{2,1,0:T(8,128)}, u32[]{:S(2)}) copy-start(f32[16,256,128]{2,1,0:T(8,128)} %copy-done.3) | copy-start | bytes 6291460
  808.0 6.1 copy-start.7
  808.0 6.1 copy-start.11
  1001.3 327.6 %all-reduce.9.cloned.1.call-start = ((), (), s32[]{:S(2)}) async-start(), calls=%async_computation.12 | async-start | bytes 131072 | tf_op jit(solution)/shard_map/psum | solution.py:145
  1307.9 3.1 copy-start.13
  (9 other events, 13.0 us)
Sparse Core Ops, SparseCore 0:
  11.3 65.9 all-gather.16
  80.6 61.4 all-gather.18
  145.5 189.7 all-gather.8
  338.5 189.9 all-gather.10
  534.2 109.9 all-reduce.4
  646.3 79.6 reduce-scatter.2
  728.2 78.1 reduce-scatter.4
  809.2 188.2 all-gather.14
  1000.2 189.7 all-gather.12
  1195.8 109.9 all-reduce.6
  1312.1 16.8 all-reduce.8
where the time goes:
time: 1350 us; the launch traced here: 1340 us
  waiting for transfers between devices  879 us (65%)
  other arithmetic  165 us (12%)
  blocking collectives  114 us (8%)
  matrix products  110 us (8%)
  local copies, waits for them, and re-layouts  54 us (4%)
  between operations  14.6 us (1%)
    all_gather x4, waiting for transfers between devices, carried_in(): lax.all_gather(a.astype(kind), axis)  562 us
    psum x2, waiting for transfers between devices, spread(): return lax.psum(kept, axis)  111 us
    all_gather x2, blocking collectives, carried_in(): lax.all_gather(a.astype(kind), axis)  109 us
    add x30, other arithmetic, combine(): latter[0][:, None, None] * earlier[1] + latter[1]  106 us
    reduce_scatter x1, waiting for transfers between devices, attention(): lax.psum_scatter(dv_all.astype(jnp.bfloat16), 'ctx', scatter_dimension=0,...  78.9 us
    all_gather x1, waiting for transfers between devices, attention(): lax.all_gather(value_states, 'ctx', axis=0, tiled=True)  64.8 us
    reduce_scatter x1, waiting for transfers between devices, attention(): lax.psum_scatter(dk_all.astype(jnp.bfloat16), 'ctx', scatter_dimension=0,...  42.3 us
  transfers between devices with their start and end apart: 11, of which 11 were waited for; matrix products, arithmetic and copies ran while one was open for 23% of the time, Pallas kernels for 0%

commit v1 on v0

--- a/solution.py
+++ b/solution.py
@@ -46,7 +46,7 @@
 
 def spread(value, axis, source):
     kept = jnp.where(lax.axis_index(axis) == source, value, 0).astype(value.dtype)
-    return lax.psum(kept, axis)
+    return jnp.sum(lax.all_gather(kept, axis), axis=0)
 
 
 def combine(earlier, latter):

time: 1350 us -> 1520 us (1.13)
  waiting for transfers between devices: 879 us -> 1050 us
    all_gather x0 -> x2, waiting for transfers between devices: none -> 289 us  [spread(): return jnp.sum(lax.all_gather(kept, axis), axis=0)]
    psum x2 -> x0, waiting for transfers between devices: 111 us -> none  [spread(): return lax.psum(kept, axis)]
    all_gather x4, waiting for transfers between devices: 562 us -> 521 us  [carried_in(): lax.all_gather(a.astype(kind), axis)]
    reduce_scatter x1, waiting for transfers between devices: 42.3 us -> 71.6 us  [attention(): lax.psum_scatter(dk_all.astype(jnp.bfloat16), 'ctx', scatter_dimension=0,...]
    add x30, other arithmetic: 106 us -> 83.8 us  [combine(): latter[0][:, None, None] * earlier[1] + latter[1]]
    reduce_sum x0 -> x2, other arithmetic: none -> 19.8 us  [spread(): return jnp.sum(lax.all_gather(kept, axis), axis=0)]
  transfers between devices with their start and end apart: 11 -> 11, of which waited for: 11 -> 11; matrix products, arithmetic and copies ran while one was open for 23% -> 19% of each run, Pallas kernels for 0% -> 0%
where the time goes in v1:
time: 1520 us; the launch traced here: 1510 us
  waiting for transfers between devices  1050 us (69%)
  other arithmetic  160 us (11%)
  blocking collectives  116 us (8%)
  matrix products  115 us (8%)
  local copies, waits for them, and re-layouts  45.9 us (3%)
    all_gather x4, waiting for transfers between devices, carried_in(): lax.all_gather(a.astype(kind), axis)  521 us
    all_gather x2, waiting for transfers between devices, spread(): return jnp.sum(lax.all_gather(kept, axis), axis=0)  289 us
    all_gather x2, blocking collectives, carried_in(): lax.all_gather(a.astype(kind), axis)  110 us
    add x30, other arithmetic, combine(): latter[0][:, None, None] * earlier[1] + latter[1]  83.8 us
    reduce_scatter x1, waiting for transfers between devices, attention(): lax.psum_scatter(dv_all.astype(jnp.bfloat16), 'ctx', scatter_dimension=0,...  78.6 us
    reduce_scatter x1, waiting for transfers between devices, attention(): lax.psum_scatter(dk_all.astype(jnp.bfloat16), 'ctx', scatter_dimension=0,...  71.6 us
    all_gather x1, waiting for transfers between devices, attention(): lax.all_gather(value_states, 'ctx', axis=0, tiled=True)  64.6 us
  transfers between devices with their start and end apart: 11, of which 11 were waited for; matrix products, arithmetic and copies ran while one was open for 19% of the time, Pallas kernels for 0%

profile of v1, /device:TPU:0, one launch (start us, length us, event | category | flops | bytes accessed | tf_op | source)
XLA Modules:
  0.0 1506.8 jit_solution(10608342710527289555)
XLA Ops:
  9.1 3.8 fusion.126
  16.4 42.5 %all-gather.2 = bf16[16,1,16]{2,1,0:T(2,128)(2,1)S(1)} all-gather(bf16[1,1,16]{2,1,0:T(2,128)(2,1)S(1)} %get-tuple-element.1035), channel_id=1, replica_groups=mesh['ctx'=16,'tp'=2] {'ctx'}, dimensions={0}, use_global_device_ids=true | all-gather | bytes 544 | tf_op jit(solution)/shard_map/all_gather | solution.py:19
  59.4 150.6 %all-gather.13.cloned.1.call-done = bf16[16,16,256,128]{3,2,1,0:T(8,128)(2,1)} async-done(((bf16[1,16,256,128]{3,2,1,0:T(8,128)(2,1)}), bf16[16,16,256,128]{3,2,1,0:T(8,128)(2,1)}) %all-gather.13.cloned.1.call-update) | async-done | bytes 16777232 | tf_op jit(solution)/shard_map/all_gather | solution.py:19
  210.3 3.7 fusion.164
  216.8 68.0 %all-gather.3 = bf16[16,1,16]{2,1,0:T(2,128)(2,1)S(1)} all-gather(bf16[1,1,16]{2,1,0:T(2,128)(2,1)S(1)} %get-tuple-element.1036), channel_id=1, replica_groups=mesh['ctx'=16,'tp'=2] {'ctx'}, dimensions={0}, use_global_device_ids=true | all-gather | bytes 544 | tf_op jit(solution)/shard_map/all_gather | solution.py:19
  288.4 115.0 %all-gather.15.cloned.1.call-done = bf16[16,16,256,128]{3,2,1,0:T(8,128)(2,1)} async-done(((bf16[1,16,256,128]{3,2,1,0:T(8,128)(2,1)}), bf16[16,16,256,128]{3,2,1,0:T(8,128)(2,1)}) %all-gather.15.cloned.1.call-update) | async-done | bytes 16777232 | tf_op jit(solution)/shard_map/all_gather | solution.py:19
  405.0 55.1 %while.95 = (s32[]{:T(128)}, f32[16]{0:T(128)S(1)}, f32[16,256,128]{2,1,0:T(8,128)}, s32[]{:T(128)}, bf16[16,16]{1,0:T(8,128)(2,1)S(1)}, /*index=5*/bf16[16,16,2...) while((s32[]{:T(128)}, f32[16]{0:T(128)S(1)}, f32[16,256,128]{2,1,0:T(8,128)}, ...), condition=%wide.region_4.5_spmd, body=%wide.region_3.4_spmd.sunk | while | flops 1572902 | bytes 5243331 | solution.py:36
  405.0 3.6 convert_add_fusion.9
  412.1 4.0 convert_add_fusion.9
  419.7 3.6 convert_add_fusion.9
  423.3 3.6 convert_add_fusion.9
  426.8 3.6 convert_add_fusion.9
  430.4 3.6 convert_add_fusion.9
  434.0 3.6 convert_add_fusion.9
  444.7 4.4 convert_add_fusion.9
  452.7 3.6 convert_add_fusion.9
  456.3 3.6 convert_add_fusion.9
  460.1 136.5 %all-gather.25.cloned.1.call-done = bf16[256,256,128]{2,1,0:T(8,128)(2,1)} async-done(((bf16[16,256,128]{2,1,0:T(8,128)(2,1)}), bf16[256,256,128]{2,1,0:T(8,128)(2,1)}) %all-gather.25.cloned.1.call-update) | async-done | bytes 16777232 | tf_op jit(solution)/shard_map/all_gather | solution.py:49
  596.6 9.9 reduce_sum.98
  624.5 4.6 fusion.135
  631.1 4.4 fusion.144
  641.7 19.5 %all-gather.21.cloned.1.call-done = bf16[2048,512]{0,1:T(8,128)(2,1)} async-done(((bf16[128,512]{0,1:T(8,128)(2,1)}), bf16[2048,512]{0,1:T(8,128)(2,1)}) %all-gather.21.cloned.1.call-update) | async-done | bytes 2097168 | tf_op jit(solution)/shard_map/all_gather | solution.py:281
  661.2 64.6 %all-gather.23.cloned.1.call-done = bf16[2048,512]{0,1:T(8,128)(2,1)} async-done(((bf16[128,512]{0,1:T(8,128)(2,1)}), bf16[2048,512]{0,1:T(8,128)(2,1)}) %all-gather.23.cloned.1.call-update) | async-done | bytes 2097168 | tf_op jit(solution)/shard_map/all_gather | solution.py:282
  726.1 28.6 %while.98 = (s32[]{:T(128)}, f32[2,4,8,64]{3,2,1,0:T(8,128)S(1)}, f32[2,4,8,64]{3,2,1,0:T(8,128)S(1)}, f32[2,4,8,64,128]{4,3,2,1,0:T(8,128)S(1)}, s32[2,64]{1,0:...) while((s32[]{:T(128)}, f32[2,4,8,64]{3,2,1,0:T(8,128)S(1)}, ...), condition=%wide.region_23.24_spmd, body=%wide.region_18.23_spmd.sunk | while | flops 2194853888 | bytes 69060272 | solution.py:235
  755.5 4.3 multiply_reduce_fusion
  765.7 66.2 %while.99 = (s32[]{:T(128)}, f32[2,64,4,8,128]{4,1,3,2,0:T(8,128)S(1)}, f32[2048,4,128]{2,0,1:T(8,128)}, f32[2048,4,128]{2,0,1:T(8,128)}, bf16[2048,512]{0,1:T(8...) while((s32[]{:T(128)}, ...), condition=%wide.region_26.27_spmd, body=%wide.region_25.26_spmd.sunk | while | flops 5417635840 | bytes 115910384 | solution.py:235
  779.2 4.5 fusion.326
  783.8 4.5 fusion.327
  788.3 5.2 fusion.328
  793.5 5.2 fusion.329
  812.0 4.5 fusion.326
  816.5 4.5 fusion.327
  821.1 5.2 fusion.328
  826.3 5.2 fusion.329
  831.9 3.8 convert_element_type.299
  835.8 3.8 convert_element_type.301
  840.4 78.5 %all-gather.19.cloned.1.call-done = bf16[16,16,256,128]{3,2,1,0:T(8,128)(2,1)} async-done(((bf16[1,16,256,128]{3,2,1,0:T(8,128)(2,1)}), bf16[16,16,256,128]{3,2,1,0:T(8,128)(2,1)}) %all-gather.19.cloned.1.call-update) | async-done | bytes 16777232 | tf_op jit(solution)/shard_map/all_gather | solution.py:19
  921.1 3.7 fusion.165
  928.3 71.6 %reduce-scatter.3.cloned.1.call-done = bf16[128,4,128]{2,0,1:T(8,128)(2,1)} async-done(((bf16[2048,4,128]{2,0,1:T(8,128)(2,1)}), bf16[128,4,128]{2,0,1:T(8,128)(2,1)}) %reduce-scatter.3.cloned.1.call-update) | async-done | bytes 131088 | tf_op jit(solution)/shard_map/reduce_scatter | solution.py:335
  1001.5 78.6 %reduce-scatter.5.cloned.1.call-done = bf16[128,4,128]{2,0,1:T(8,128)(2,1)} async-done(((bf16[2048,4,128]{2,0,1:T(8,128)(2,1)}), bf16[128,4,128]{2,0,1:T(8,128)(2,1)}) %reduce-scatter.5.cloned.1.call-update) | async-done | bytes 131088 | tf_op jit(solution)/shard_map/reduce_scatter | solution.py:338
  1081.6 6.1 fusion.158
  1091.2 4.7 fusion.150
  1095.9 176.4 %all-gather.17.cloned.1.call-done = bf16[16,16,256,128]{3,2,1,0:T(8,128)(2,1)} async-done(((bf16[1,16,256,128]{3,2,1,0:T(8,128)(2,1)}), bf16[16,16,256,128]{3,2,1,0:T(8,128)(2,1)}) %all-gather.17.cloned.1.call-update) | async-done | bytes 16777232 | tf_op jit(solution)/shard_map/all_gather | solution.py:19
  1272.5 40.1 %while.96 = (s32[]{:T(128)}, f32[16]{0:T(128)S(1)}, f32[16,256,128]{2,1,0:T(8,128)S(1)}, s32[]{:T(128)}, bf16[16,16]{1,0:T(8,128)(2,1)}, /*index=5*/bf16[16,16,2...) while((s32[]{:T(128)}, f32[16]{0:T(128)S(1)}, f32[16,256,128]{2,1,0:T(8,128)S(1)}, ...), condition=%wide.region_11.12_spmd, body=%wide.region_10.11_spmd.sunk | while | flops 1572902 | bytes 5243331 | solution.py:36
  1312.7 152.1 %all-gather.27.cloned.1.call-done = bf16[256,256,128]{2,1,0:T(8,128)(2,1)} async-done(((bf16[16,256,128]{2,1,0:T(8,128)(2,1)}), bf16[256,256,128]{2,1,0:T(8,128)(2,1)}) %all-gather.27.cloned.1.call-update) | async-done | bytes 16777232 | tf_op jit(solution)/shard_map/all_gather | solution.py:49
  1464.8 9.9 reduce_sum.101
  1481.2 6.3 fusion.138
  1489.6 7.8 all-reduce.3.cloned.1.call-done
  (277 shorter events, 183.5 us)
Async XLA Ops:
  7.2 277.7 %copy-start = (bf16[128,128]{1,0:T(8,128)(2,1)S(1)}, bf16[128,128]{1,0:T(8,128)(2,1)}, u32[]{:S(2)}) copy-start(bf16[128,128]{1,0:T(8,128)(2,1)} %param.31) | copy-start | bytes 98308
  7.2 1.6 copy-start.38
  7.2 1.9 copy-start.22
  7.2 202.9 %all-gather.13.cloned.1.call-start = ((), (), s32[]{:S(2)}) async-start(), calls=%async_computation.2 | async-start | bytes 17825792 | tf_op jit(solution)/shard_map/all_gather | solution.py:19
  8.7 600.1 %copy-start.7 = (bf16[16,8,16,256]{3,2,1,0:T(8,128)(2,1)}, bf16[16,8,16,256]{3,2,1,0:T(8,128)(2,1)S(1)}, u32[]{:S(2)}) copy-start(bf16[16,8,16,256]{3,2,1,0:T(8,128)(2,1)S(1)} %copy.150) | copy-start | bytes 3145732
  9.1 3.8 copy-start.26
  12.9 2.6 copy-start.12
  15.6 387.8 %all-gather.15.cloned.1.call-start = ((), (), s32[]{:S(2)}) async-start(), calls=%async_computation.3 | async-start | bytes 17825792 | tf_op jit(solution)/shard_map/all_gather | solution.py:19
  16.3 580.3 %all-gather.25.cloned.1.call-start = ((), (), s32[]{:S(2)}) async-start(), calls=%async_computation.10 | async-start | bytes 17825792 | tf_op jit(solution)/shard_map/all_gather | solution.py:49
  210.3 3.8 copy-start.34
  210.3 398.5 %copy-start.1 = (f32[16,256,128]{2,1,0:T(8,128)}, f32[16,256,128]{2,1,0:T(8,128)S(1)}, u32[]{:S(2)}) copy-start(f32[16,256,128]{2,1,0:T(8,128)S(1)} %get-tuple-element.852) | copy-start | bytes 6291460
  210.3 3.8 copy-start.30
  214.1 447.1 %all-gather.21.cloned.1.call-start = ((), (), s32[]{:S(2)}) async-start(), calls=%async_computation.6 | async-start | bytes 2228224 | tf_op jit(solution)/shard_map/all_gather | solution.py:281
  215.0 510.8 %all-gather.23.cloned.1.call-start = ((), (), s32[]{:S(2)}) async-start(), calls=%async_computation.7 | async-start | bytes 2228224 | tf_op jit(solution)/shard_map/all_gather | solution.py:282
  216.7 702.2 %all-gather.19.cloned.1.call-start = ((), (), s32[]{:S(2)}) async-start(), calls=%async_computation.5 | async-start | bytes 17825792 | tf_op jit(solution)/shard_map/all_gather | solution.py:19
  216.8 188.2 %copy-start.31 = (pred[64,64]{1,0:T(8,128)(4,1)}, pred[64,64]{1,0:T(8,128)(4,1)S(1)}, u32[]{:S(2)}) copy-start(pred[64,64]{1,0:T(8,128)(4,1)S(1)} %iota_compare_fusion) | copy-start | bytes 12292
  216.8 188.1 %copy-start.24 = (f32[2,16,64]{2,1,0:T(8,128)}, f32[2,16,64]{2,1,0:T(8,128)S(1)}, u32[]{:S(2)}) copy-start(f32[2,16,64]{2,1,0:T(8,128)S(1)} %copy.79) | copy-start | bytes 24580
  284.9 344.9 %copy-start.28 = (f32[2,64,16]{1,2,0:T(8,128)}, f32[2,64,16]{1,2,0:T(8,128)S(1)}, u32[]{:S(2)}) copy-start(f32[2,64,16]{1,2,0:T(8,128)S(1)} %copy.82) | copy-start | bytes 24580
  460.1 146.4 %copy-start.35 = (bf16[16,16]{1,0:T(8,128)(2,1)}, bf16[16,16]{1,0:T(8,128)(2,1)S(1)}, u32[]{:S(2)}) copy-start(bf16[16,16]{1,0:T(8,128)(2,1)S(1)} %get-tuple-element.1601) | copy-start | bytes 1540
  606.5 2.6 copy-start.15
  606.5 2.6 copy-start.36
  608.8 3.5 copy-start.9
  613.5 1.7 copy-start.14
  615.2 3.2 copy-start.33
  635.5 2.7 copy-start.11
  635.5 2.8 copy-start.17
  638.2 361.7 %reduce-scatter.3.cloned.1.call-start = ((), (), s32[]{:S(2)}) async-start(), calls=%async_computation.8 | async-start | bytes 2228224 | tf_op jit(solution)/shard_map/reduce_scatter | solution.py:335
  638.6 1.6 copy-start.13
  767.6 1.5 copy-start.19
  800.4 1.5 copy-start.19
  835.8 244.3 %reduce-scatter.5.cloned.1.call-start = ((), (), s32[]{:S(2)}) async-start(), calls=%async_computation.9 | async-start | bytes 2228224 | tf_op jit(solution)/shard_map/reduce_scatter | solution.py:338
  839.6 432.7 %all-gather.17.cloned.1.call-start = ((), (), s32[]{:S(2)}) async-start(), calls=%async_computation.4 | async-start | bytes 17825792 | tf_op jit(solution)/shard_map/all_gather | solution.py:19
  840.4 624.4 %all-gather.27.cloned.1.call-start = ((), (), s32[]{:S(2)}) async-start(), calls=%async_computation.11 | async-start | bytes 17825792 | tf_op jit(solution)/shard_map/all_gather | solution.py:49
  921.1 3.8 copy-start.16
  924.8 572.5 %all-reduce.3.cloned.1.call-start = ((), (), s32[]{:S(2)}) async-start(), calls=%async_computation.12 | async-start | bytes 131072 | tf_op jit(solution)/shard_map/psum | solution.py:145
  926.4 155.3 %copy-start.2 = (f32[16,256,128]{2,1,0:T(8,128)S(1)}, f32[16,256,128]{2,1,0:T(8,128)}, u32[]{:S(2)}) copy-start(f32[16,256,128]{2,1,0:T(8,128)} %copy-done.1) | copy-start | bytes 6291460
  926.4 155.2 %copy-start.29 = (f32[2,64,16]{1,2,0:T(8,128)S(1)}, f32[2,64,16]{1,2,0:T(8,128)}, u32[]{:S(2)}) copy-start(f32[2,64,16]{1,2,0:T(8,128)} %copy-done.28) | copy-start | bytes 24580
  1081.6 6.1 copy-start.6
  1081.6 6.1 copy-start.8
  1081.6 6.2 copy-start.25
  1081.6 6.1 copy-start.32
  1087.8 2.6 copy-start.23
  1087.8 3.4 copy-start.21
  1312.6 162.0 %copy-start.4 = (f32[16,256,128]{2,1,0:T(8,128)}, f32[16,256,128]{2,1,0:T(8,128)S(1)}, u32[]{:S(2)}) copy-start(f32[16,256,128]{2,1,0:T(8,128)S(1)} %get-tuple-element.857) | copy-start | bytes 6291460
  1474.7 2.5 copy-start.3
  1474.7 2.5 copy-start.27
  1477.0 3.3 copy-start.10
  1477.2 4.0 copy-start.37
  (4 other events, 3.9 us)
Sparse Core Ops, SparseCore 0:
  15.7 194.3 all-gather.12
  213.4 189.9 all-gather.14
  406.7 189.7 all-gather.24
  599.7 61.4 all-gather.20
  664.3 61.4 all-gather.22
  729.0 189.8 all-gather.18
  921.2 78.6 reduce-scatter.2
  1002.2 77.8 reduce-scatter.4
  1083.4 188.8 all-gather.16
  1274.9 189.7 all-gather.26
  1481.3 15.9 all-reduce.2
